TPU v7x, 32 devices: a whole 2x2x4 slice. The times are simulated.
32 devices in a mesh: seq: 16 (over z, y, core), head: 2 (over x).
Axes of the slice: x: 2, y: 2, z: 4, core: 2. Of those that a mesh axis runs over, the one named last changes fastest.
Arguments:
- volume: bfloat16 [8192, 64], P('seq'), may hold values from -6 to 6
- vox_mask: int32 [8192, 64], P('seq'), may hold values 0 or 1
- embed: bfloat16 [64, 1024], replicated, may hold values from -0.75 to 0.75
- w_qkv: bfloat16 [3, 1024, 1024], P(None, None, 'head'), may hold values from -5 to 5
- w_out: bfloat16 [1024, 1024], P(None, 'head'), may hold values from -0.1875 to 0.1875
- w_head: bfloat16 [1024, 64], replicated, may hold values from -0.1875 to 0.1875
Outputs:
- grad_qkv: float32 [3, 1024, 1024], P(None, 'seq', 'head')
- grad_out: float32 [1024, 1024], P('seq', 'head')
All inputs are finite; a program needn't handle non-finite values. No bound on the sum of `vox_mask` on one device may be relied on, other than what follows from the above.
Results may differ from a plain program's by a relative error of at most 0.0038.
Values may be sent and summed in bfloat16 or wider, within the bound.
No kernel may reach another device: no remote copies, remote signals or barrier semaphores. Data moves between devices by JAX's collectives and lax.ppermute only.
A program may use at most 64 MiB of HBM per device.

v0:
```python
import math

import jax
import jax.numpy as jnp
from jax import lax
from jax.sharding import PartitionSpec as P

D = 1024
HEADS = 16
LEVELS = 2


def partner(shard, axis, apart):
    return lax.ppermute(shard, axis, [(i, i ^ 1 << apart) for i in range(lax.axis_size(axis))])


def head_major(rows, head_dim):
    return rows.reshape(rows.shape[0], rows.shape[1] // head_dim, head_dim).transpose(1, 0, 2)


def token_major(blocks):
    return blocks.transpose(1, 0, 2).reshape(blocks.shape[1], blocks.shape[0] * blocks.shape[2])


def softmax_rows(query_head, key_head, factor):
    scores = (
        jnp.einsum("qd,kd->qk", query_head, key_head, preferred_element_type=jnp.float32) * factor
    )
    highest = jnp.max(scores, -1, keepdims=True)
    raised = jnp.exp(scores - highest)
    return raised / jnp.sum(raised, -1, keepdims=True)


def per_device(volume, vox_mask, embed, w_qkv, w_out, w_head):
    tok_rows = volume.shape[0]
    head_dim = D // HEADS
    factor = head_dim ** (-0.5)
    seq_devices = lax.axis_size("seq")
    kept = volume * (1 - vox_mask).astype(jnp.bfloat16)
    hidden = jnp.dot(kept, embed, preferred_element_type=jnp.float32)
    normed = (hidden * lax.rsqrt(jnp.mean(hidden * hidden, -1, keepdims=True) + 1e-06)).astype(
        jnp.bfloat16
    )
    projected = jnp.einsum("td,jdc->jtc", normed, w_qkv, preferred_element_type=jnp.float32).astype(
        jnp.bfloat16
    )
    remote = [partner(projected[1:], "seq", level_bit) for level_bit in range(LEVELS)]
    key_rows = jnp.concatenate([projected[1]] + [other[0] for other in remote], 0)
    value_rows = jnp.concatenate([projected[2]] + [other[1] for other in remote], 0)
    query_heads = head_major(projected[0], head_dim)
    key_heads = head_major(key_rows, head_dim)
    value_heads = head_major(value_rows, head_dim)

    def forward_head(operands):
        query_head, key_head, value_head = operands
        weights = softmax_rows(query_head, key_head, factor).astype(jnp.bfloat16)
        return jnp.dot(weights, value_head, preferred_element_type=jnp.float32).astype(jnp.bfloat16)

    context_heads = lax.map(forward_head, (query_heads, key_heads, value_heads))
    context = token_major(context_heads)
    partial_out = jnp.einsum("tc,oc->to", context, w_out, preferred_element_type=jnp.float32)
    mixed = lax.psum(partial_out.astype(jnp.bfloat16), "head").astype(jnp.float32)
    stream = (hidden + mixed).astype(jnp.bfloat16)
    predicted = jnp.dot(stream, w_head, preferred_element_type=jnp.float32)
    loss_weight = 256.0 / math.sqrt(tok_rows * seq_devices)
    grad_pred = (
        vox_mask.astype(jnp.float32) * (predicted - volume.astype(jnp.float32)) * loss_weight
    ).astype(jnp.bfloat16)
    grad_stream = jnp.einsum(
        "tv,dv->td", grad_pred, w_head, preferred_element_type=jnp.float32
    ).astype(jnp.bfloat16)
    grad_context = jnp.dot(grad_stream, w_out, preferred_element_type=jnp.float32).astype(
        jnp.bfloat16
    )

    def backward_head(operands):
        query_head, key_head, value_head, context_head, grad_head = operands
        probs = softmax_rows(query_head, key_head, factor)
        grad_probs = jnp.einsum(
            "qd,kd->qk", grad_head, value_head, preferred_element_type=jnp.float32
        )
        offsets = jnp.sum(
            grad_head.astype(jnp.float32) * context_head.astype(jnp.float32), -1, keepdims=True
        )
        grad_scores = (probs * (grad_probs - offsets) * factor).astype(jnp.bfloat16)
        grad_query = jnp.dot(grad_scores, key_head, preferred_element_type=jnp.float32).astype(
            jnp.bfloat16
        )
        grad_key = jnp.einsum(
            "qk,qd->kd", grad_scores, query_head, preferred_element_type=jnp.float32
        ).astype(jnp.bfloat16)
        grad_value = jnp.einsum(
            "qk,qd->kd", probs.astype(jnp.bfloat16), grad_head, preferred_element_type=jnp.float32
        ).astype(jnp.bfloat16)
        return (grad_query, grad_key, grad_value)

    grad_q_heads, grad_k_heads, grad_v_heads = lax.map(
        backward_head,
        (query_heads, key_heads, value_heads, context_heads, head_major(grad_context, head_dim)),
    )
    grad_query = token_major(grad_q_heads)
    local_width = grad_query.shape[1]
    blocks_all = LEVELS + 1
    grad_keys = token_major(grad_k_heads).reshape(blocks_all, tok_rows, local_width)
    grad_values = token_major(grad_v_heads).reshape(blocks_all, tok_rows, local_width)
    returned = [
        partner(jnp.stack([grad_keys[level_bit + 1], grad_values[level_bit + 1]]), "seq", level_bit)
        for level_bit in range(LEVELS)
    ]
    own_keys = jnp.stack([grad_keys[0]] + [other[0] for other in returned])
    own_values = jnp.stack([grad_values[0]] + [other[1] for other in returned])
    source = normed
    query_term = jnp.einsum("tr,tc->rc", source, grad_query, preferred_element_type=jnp.float32)
    source = normed
    key_term = jnp.einsum("tr,jtc->rc", source, own_keys, preferred_element_type=jnp.float32)
    value_term = jnp.einsum("tr,jtc->rc", source, own_values, preferred_element_type=jnp.float32)
    key_term, value_term = (key_term, value_term)
    out_term = jnp.einsum("tr,tc->rc", grad_stream, context, preferred_element_type=jnp.float32)
    summed = lax.psum_scatter(
        jnp.stack([query_term, key_term, value_term, out_term], 1),
        "seq",
        scatter_dimension=0,
        tiled=True,
    )
    return (jnp.transpose(summed[:, :3, :], (1, 0, 2)), summed[:, 3, :])


def solution(mesh):
    return jax.shard_map(
        per_device,
        mesh=mesh,
        in_specs=(P("seq", None), P("seq", None), P(), P(None, None, "head"), P(None, "head"), P()),
        out_specs=(P(None, "seq", "head"), P("seq", "head")),
        check_vma=False,
    )
```

profile of v0, /device:TPU:0, one launch (start us, length us, event | category | flops | bytes accessed | tf_op | source)
XLA Modules:
  0.0 395.8 jit_solution(14222275033119210577)
XLA Ops:
  13.9 2.5 collective-permute-start.1
  18.8 2.2 fusion.67
  22.6 17.9 %collective-permute-done.1 = bf16[2,512,512]{1,2,0:T(8,128)(2,1)} collective-permute-done((bf16[2,512,512]{1,2,0:T(8,128)(2,1)}, bf16[2,512,512]{1,2,0:T(8,128)(2,1)}, u32[]{:S(2)}, u32[]{:S(2)}) %collective-permute-start.1) | collective-permute-done | bytes 1048608 | tf_op jit(solution)/shard_map/ppermute | solution.py:14
  40.5 2.3 fusion.68
  42.8 2.4 copy.22
  45.2 2.3 copy.24
  47.5 2.4 copy.25
  49.9 4.6 %maximum_bitcast_fusion = (bf16[8,1536,64]{2,1,0:T(8,128)(2,1)}, bf16[8,1536,64]{2,1,0:T(8,128)(2,1)}) fusion(bf16[512,8,64]{2,0,1:T(8,128)(2,1)} %copy.22, bf16[512,8,64]{2,0,1:T(8,128)(2,1)S(1)} %copy.21, bf16[512,8,64]{2,0,1:T(8,128)(2,1)S(1)} %copy.20, bf16[512,8,64]{2,0,1:T(8,128)(2,1)} %copy.25, bf16[512,8,64]{2,0,1:T(8,128)(2,1)} %copy.24, ...), kind=kLoop, calls=%fused_computation.57 | loop fusion | flops 9437184 | bytes 6291456 | tf_op jit(solution)/shard_map/transpose | solution.py:18
  55.3 37.6 %while.24 = (s32[]{:T(128)}, bf16[8,512,64]{1,2,0:T(8,128)(2,1)}, bf16[8,512,64]{2,1,0:T(8,128)(2,1)}, bf16[8,1536,64]{2,1,0:T(8,128)(2,1)}, bf16[8,1536,64]{2,1,0:T(8,128)(2,1)}, /*index=5*/s32[]{:T(128)}) while((s32[]{:T(128)}, bf16[8,512,64]{1,2,0:T(8,128)(2,1)}, bf16[8,512,64]{2,1,0:T(8,128)(2,1)}, bf16[8,1536,64]{2,1,0:T(8,128)(2,1)}, ...), condition=%wide.region_4.5_spmd, body=%wide.region_1.4_spmd.sunk | while | flops 206863360 | bytes 10432581 | solution.py:59
  57.6 2.4 fusion.109
  62.3 2.4 fusion.109
  67.0 2.4 fusion.109
  71.7 2.4 fusion.109
  76.4 2.4 fusion.109
  81.1 2.4 fusion.109
  85.8 2.4 fusion.109
  90.5 2.4 fusion.109
  92.9 3.3 convolution_convert_fusion.5
  96.5 41.5 %all-reduce.2.cloned.1.call-done = bf16[512,1024]{1,0:T(8,128)(2,1)} async-done(((bf16[512,1024]{1,0:T(8,128)(2,1)}), bf16[512,1024]{1,0:T(8,128)(2,1)}) %all-reduce.2.cloned.1.call-update) | async-done | bytes 1048592 | tf_op jit(solution)/shard_map/psum | solution.py:62
  138.0 2.1 convolution_convert_fusion.4
  140.1 2.4 convolution_convert_fusion.6
  144.7 103.3 %while.25 = (s32[]{:T(128)}, bf16[8,512,64]{1,2,0:T(8,128)(2,1)}, bf16[8,1536,64]{1,2,0:T(8,128)(2,1)}, bf16[8,1536,64]{1,2,0:T(8,128)(2,1)}, bf16[8,512,64]{2,1...) while((s32[]{:T(128)}, bf16[8,512,64]{1,2,0:T(8,128)(2,1)}, ...), condition=%wide.region_10.11_spmd, body=%wide.region_6.10_spmd.sunk | while | flops 513899008 | bytes 19881068 | solution.py:97
  147.0 2.3 fusion.124
  153.4 2.0 fusion.123
  155.4 2.2 fusion.122
  159.9 2.3 fusion.124
  168.3 2.2 fusion.122
  172.8 2.3 fusion.124
  179.2 2.0 fusion.123
  181.2 2.2 fusion.122
  185.7 2.3 fusion.124
  192.1 2.0 fusion.123
  194.1 2.2 fusion.122
  198.6 2.3 fusion.124
  205.0 2.0 fusion.123
  207.1 2.2 fusion.122
  211.6 2.3 fusion.124
  217.9 2.0 fusion.123
  220.0 2.2 fusion.122
  224.5 2.3 fusion.124
  230.9 2.0 fusion.123
  232.9 2.2 fusion.122
  237.4 2.3 fusion.124
  243.8 2.0 fusion.123
  245.8 2.2 fusion.122
  255.5 20.4 %collective-permute-done.3 = bf16[2,512,512]{1,2,0:T(8,128)(2,1)S(1)} collective-permute-done((bf16[2,512,512]{1,2,0:T(8,128)(2,1)S(1)}, bf16[2,512,512]{1,2,0:T(8,128)(2,1)S(1)}, u32[]{:S(2)}, u32[]{:S(2)}) %collective-permute-start.3) | collective-permute-done | bytes 1048608 | tf_op jit(solution)/shard_map/ppermute | solution.py:14
  278.0 4.0 pad_maximum_fusion
  282.0 103.6 %reduce-scatter.2.cloned.1.call-done = f32[64,4,512]{2,0,1:T(8,128)} async-done(((f32[1024,4,512]{2,0,1:T(8,128)}), f32[64,4,512]{2,0,1:T(8,128)}) %reduce-scatter.2.cloned.1.call-update) | async-done | bytes 524304 | tf_op jit(solution)/shard_map/reduce_scatter | solution.py:119
  (127 shorter events, 97.6 us)
Async XLA Ops:
  7.2 3.3 copy-start
  7.2 130.8 %all-reduce.2.cloned.1.call-start = ((), (), s32[]{:S(2)}) async-start(), calls=%async_computation.1 | async-start | bytes 2097152 | tf_op jit(solution)/shard_map/psum | solution.py:62
  8.9 1.4 copy-start.2
  10.5 1.9 copy-start.4
  13.4 5.4 %collective-permute-start = (bf16[2,512,512]{1,2,0:T(8,128)(2,1)}, bf16[2,512,512]{1,2,0:T(8,128)(2,1)}, u32[]{:S(2)}, u32[]{:S(2)}) collective-permute-start(bf16[2,512,512]{1,2,0:T(8,128)(2,1)} %slice.107), channel_id=1, source_target_pairs={{0,2},{2,0},{4,6},{6,4},{8,10},{10,8},{12,14},{14,12},{16,18},{18,... | collective-permute-start | bytes 3145736 | tf_op jit(solution)/shard_map/ppermute | solution.py:14
  13.9 26.6 %collective-permute-start.1 = (bf16[2,512,512]{1,2,0:T(8,128)(2,1)}, bf16[2,512,512]{1,2,0:T(8,128)(2,1)}, u32[]{:S(2)}, u32[]{:S(2)}) collective-permute-start(bf16[2,512,512]{1,2,0:T(8,128)(2,1)} %slice.107), channel_id=1, source_target_pairs={{0,4},{2,6},{4,0},{6,2},{8,12},{10,14},{12,8},{14,10},{16,20},{18,... | collective-permute-start | bytes 3145736 | tf_op jit(solution)/shard_map/ppermute | solution.py:14
  92.9 45.1 %copy-start.3 = (f32[512,1024]{1,0:T(8,128)S(1)}, f32[512,1024]{1,0:T(8,128)}, u32[]{:S(2)}) copy-start(f32[512,1024]{1,0:T(8,128)} %copy-done.2) | copy-start | bytes 6291460
  92.9 45.1 %copy-start.9 = (s32[512,64]{0,1:T(8,128)S(1)}, s32[512,64]{0,1:T(8,128)}, u32[]{:S(2)}) copy-start(s32[512,64]{0,1:T(8,128)} %param.11) | copy-start | bytes 393220
  92.9 45.1 %copy-start.10 = (bf16[1024,64]{0,1:T(8,128)(2,1)S(1)}, bf16[1024,64]{0,1:T(8,128)(2,1)}, u32[]{:S(2)}) copy-start(bf16[1024,64]{0,1:T(8,128)(2,1)} %param.15) | copy-start | bytes 393220
  92.9 45.1 %copy-start.11 = (bf16[512,64]{0,1:T(8,128)(2,1)S(1)}, bf16[512,64]{0,1:T(8,128)(2,1)}, u32[]{:S(2)}) copy-start(bf16[512,64]{0,1:T(8,128)(2,1)} %param.10) | copy-start | bytes 196612
  96.3 289.3 %reduce-scatter.2.cloned.1.call-start = ((), (), s32[]{:S(2)}) async-start(), calls=%async_computation.2 | async-start | bytes 8912896 | tf_op jit(solution)/shard_map/reduce_scatter | solution.py:119
  140.1 4.6 %copy-start.6 = (bf16[512,1024]{1,0:T(8,128)(2,1)}, bf16[512,1024]{1,0:T(8,128)(2,1)S(1)}, u32[]{:S(2)}) copy-start(bf16[512,1024]{1,0:T(8,128)(2,1)S(1)} %convolution_convert_fusion.4) | copy-start | bytes 3145732
  248.0 1.9 copy-start.8
  249.9 2.0 copy-start.7
  250.1 3.6 copy-start.5
  250.1 5.4 %collective-permute-start.2 = (bf16[2,512,512]{1,2,0:T(8,128)(2,1)S(1)}, bf16[2,512,512]{1,2,0:T(8,128)(2,1)S(1)}, u32[]{:S(2)}, u32[]{:S(2)}) collective-permute-start(bf16[2,512,512]{1,2,0:T(8,128)(2,1)S(1)} %pad_maximum_fusion.1), channel_id=1, source_target_pairs={{0,2},{2,0},{4,6},{6,4},{8,10},{10,8},{12,14},{14,12},{16,18},{18,... | collective-permute-start | bytes 3145736 | tf_op jit(solution)/shard_map/ppermute | solution.py:14
  250.3 25.6 %collective-permute-start.3 = (bf16[2,512,512]{1,2,0:T(8,128)(2,1)S(1)}, bf16[2,512,512]{1,2,0:T(8,128)(2,1)S(1)}, u32[]{:S(2)}, u32[]{:S(2)}) collective-permute-start(bf16[2,512,512]{1,2,0:T(8,128)(2,1)S(1)} %pad_maximum_fusion.2), channel_id=1, source_target_pairs={{0,4},{2,6},{4,0},{6,2},{8,12},{10,14},{12,8},{14,10},{16,20},{18,... | collective-permute-start | bytes 3145736 | tf_op jit(solution)/shard_map/ppermute | solution.py:14
  282.0 107.0 %copy-start.1 = (bf16[3,1024,512]{2,1,0:T(8,128)(2,1)S(1)}, bf16[3,1024,512]{2,1,0:T(8,128)(2,1)}, u32[]{:S(2)}) copy-start(bf16[3,1024,512]{2,1,0:T(8,128)(2,1)} %param.13) | copy-start | bytes 9437188
Sparse Core Ops, SparseCore 0:
  96.4 41.5 all-reduce.1
  282.1 103.4 reduce-scatter.1
where the time goes:
time: 398 us; the launch traced here: 396 us
  waiting for transfers between devices  183 us (46%)
  matrix products  132 us (33%)
  local copies, waits for them, and re-layouts  34.2 us (9%)
  other arithmetic  27 us (7%)
  between operations  14.3 us (4%)
  starting transfers between devices  4.87 us (1%)
    reduce_scatter x1, waiting for transfers between devices, per_device(): lax.psum_scatter(jnp.stack([query_term, key_term, value_term, out_term],...  104 us
    psum x1, waiting for transfers between devices, per_device(): lax.psum(partial_out.astype(jnp.bfloat16), 'head').astype(jnp.float32)  41.5 us
    ppermute x4, waiting for transfers between devices, partner(): lax.ppermute(shard, axis, [(i, i ^ 1 << apart) for i in range(lax.axis_si...  38.3 us
    dot_general x16, matrix products, softmax_rows(): jnp.einsum('qd,kd->qk', query_head, key_head, preferred_element_type=jnp....  27.6 us
    dot_general x8, matrix products, forward_head(): jnp.dot(weights, value_head, preferred_element_type=jnp.float32)  19.2 us
    dot_general x8, matrix products, backward_head(): jnp.einsum('qk,qd->kd', probs.astype(jnp.bfloat16), grad_head, preferred_...  18.7 us
    dot_general x8, matrix products, backward_head(): jnp.dot(grad_scores, key_head, preferred_element_type=jnp.float32)  17.7 us
    dot_general x8, matrix products, backward_head(): jnp.einsum('qk,qd->kd', grad_scores, query_head, preferred_element_type=j...  16.2 us
  transfers between devices with their start and end apart: 6, of which 4 were waited for; matrix products, arithmetic and copies ran while one was open for 3% of the time, Pallas kernels for 0%

commit v1 on v0

v1 whole, which is shorter than its diff:
```python
import functools
import math

import jax
import jax.numpy as jnp
from jax import lax
from jax.experimental import pallas as pl
from jax.experimental.pallas import tpu as pltpu
from jax.sharding import PartitionSpec as P

HEADS = 16
LEVELS = 2
F32 = jnp.float32
BF16 = jnp.bfloat16
VMEM = pltpu.MemorySpace.VMEM


def dot(a, b):
    return jnp.dot(a, b, preferred_element_type=F32)


def dot_nt(a, b, precision=None):
    return lax.dot_general(a, b, (((1,), (1,)), ((), ())), precision, F32)


def dot_tn(a, b, precision=None):
    return lax.dot_general(a, b, (((0,), (0,)), ((), ())), precision, F32)


def split(x):
    high = x.astype(BF16)
    return high, (x - high.astype(F32)).astype(BF16)


def low_half(shape, width):
    return lax.broadcasted_iota(jnp.int32, shape, 1) < width


def half_masks(pair, width):
    left = low_half(pair.shape, width)
    return jnp.where(left, pair, 0.0), jnp.where(left, 0.0, pair)


HIGH = lax.Precision.HIGHEST


def weights_kernel(
    scale, embed_ref, w_qkv_ref, w_out_ref, w_head_ref, b4_ref, a2_ref, ah_ref, terms_ref, own_ref
):
    vox = embed_ref.shape[0]
    pair = 2 * vox
    embed = embed_ref[...]
    eq = dot(embed, w_qkv_ref[0])
    ek = dot(embed, w_qkv_ref[1])
    ev = dot(embed, w_qkv_ref[2])
    gt = dot_tn(w_head_ref[...], w_out_ref[...])
    terms_ref[0] = eq
    terms_ref[1] = ek
    terms_ref[2] = ev
    terms_ref[3] = gt
    own = dot(embed, w_head_ref[...])
    own_hi, own_lo = split(own)
    own_ref[...] = jnp.concatenate([own_hi, own_lo], 0)
    for p in range(eq.shape[1] // pair):
        cols = slice(p * pair, (p + 1) * pair)
        ke, ko = half_masks(ek[:, cols], vox)
        b = dot_nt(eq[:, cols] * scale, jnp.concatenate([ke, ke, ko, ko], 0), HIGH)
        hi, lo = split(b)
        wide = slice(2 * p * pair, 2 * (p + 1) * pair)
        b4_ref[:, wide] = jnp.concatenate([hi, hi, lo, lo], 0)
        ve, vo = half_masks(ev[:, cols], vox)
        a = dot_nt(gt[:, cols], jnp.concatenate([ve, ve, vo, vo], 0), HIGH)
        hi, lo = split(a)
        a2_ref[:, wide] = jnp.concatenate([hi, lo], 0)
        plain = jnp.where(low_half((vox, pair), vox), a[:, :pair], a[:, pair:])
        hi, lo = split(plain)
        ah_ref[:, cols] = jnp.concatenate([hi, lo], 0)


def forward_kernel(
    kept_ref, k1_ref, k2_ref, embed_ref, b4_ref, ah_ref,
    e_ref, c_ref, inv_ref, part_ref, u2_ref, qt_ref,
    ut_ref, ur_ref, q_ref,
):
    step = pl.program_id(0)
    rows, vox = kept_ref.shape
    pair = 2 * vox
    dim = embed_ref.shape[1]

    @pl.when(step == 0)
    def _():
        for j, ref in enumerate((kept_ref, k1_ref, k2_ref)):
            kept = ref[...]
            hidden = dot(kept, embed_ref[...])
            rms = lax.rsqrt(jnp.sum(hidden * hidden, -1, keepdims=True) / dim + 1e-06)
            u = kept.astype(F32) * rms
            hi = u.astype(BF16).astype(F32)
            both = jnp.concatenate([hi, u - hi], 1)
            both_b = both.astype(BF16)
            here = slice(j * rows, (j + 1) * rows)
            u2_ref[here, :] = both_b
            ur_ref[here, :pair] = both_b
            ur_ref[here, pair:] = jnp.ones((rows, pair), BF16)
            flipped = both.T.astype(BF16)
            ut_ref[:, here] = flipped
            if j == 0:
                qt_ref[...] = flipped
                q_ref[...] = dot(jnp.concatenate([both_b, both_b], 1), b4_ref[...]).astype(BF16)

    both_c = []
    for i in range(2):
        q = q_ref[:, pl.ds(pl.multiple_of((2 * step + i) * pair, pair), pair)]
        s = dot(q, ut_ref[...])
        e = jnp.exp2(s - jnp.max(s, -1, keepdims=True)).astype(BF16)
        e_ref[i] = e
        c2 = dot(e, ur_ref[...])
        inv = 1.0 / c2[:, pair:]
        c = c2[:, :pair]
        both_c.append((c + pltpu.roll(c, vox, 1)) * inv)
        inv_ref[i] = inv
    here = pl.ds(pl.multiple_of(step * pair, pair), pair)
    c = jnp.where(low_half((rows, pair), vox), both_c[0], both_c[1])
    c_ref[:, here] = c
    hi, lo = split(c)
    ah = ah_ref[:, here]
    p2 = dot_nt(hi, ah)
    term = p2[:, :vox] + p2[:, vox:] + dot_nt(lo, ah)[:, :vox]

    @pl.when(step == 0)
    def _():
        part_ref[...] = term

    @pl.when(step > 0)
    def _():
        part_ref[...] += term


def backward_kernel(
    loss_weight, factor,
    part_ref, other_ref, vol_ref, mask_ref, kept_ref, own_ref, a2_ref, c_ref, inv_ref, e_ref, u2_ref, qt_ref,
    m_ref, n_ref,
    ut_ref, a_ref,
):
    step = pl.program_id(0)
    rows, vox = vol_ref.shape
    pair = 2 * vox
    keys = u2_ref.shape[0]

    @pl.when(step == 0)
    def _():
        kept = kept_ref[...]
        own = dot(jnp.concatenate([kept, kept], 1), own_ref[...])
        predicted = own + (part_ref[...] + other_ref[...])
        gp = (mask_ref[...].astype(F32) * (predicted - vol_ref[...].astype(F32)) * loss_weight).astype(BF16)
        a_ref[...] = dot(jnp.concatenate([gp, gp], 1), a2_ref[...]).astype(BF16)
        hi, lo = split(c_ref[...])
        n_ref[...] = dot_tn(gp, hi) + dot_tn(gp, lo)
        for j in range(keys // rows):
            here = slice(j * rows, (j + 1) * rows)
            ut_ref[:pair, here] = u2_ref[here, :].astype(F32).T.astype(BF16)
        row = lax.broadcasted_iota(jnp.int32, (pair, keys), 0)
        ut_ref[pair:, :] = jnp.where(row < 2, -1.0, 0.0).astype(BF16)

    here = pl.ds(pl.multiple_of(step * pair, pair), pair)
    c = c_ref[:, here]
    masked = half_masks(c, vox)
    lane = lax.broadcasted_iota(jnp.int32, (rows, pair), 1)
    xs = []
    for i in range(2):
        a = a_ref[:, pl.ds(pl.multiple_of((2 * step + i) * pair, pair), pair)]
        off = jnp.sum(a.astype(F32) * masked[i], -1, keepdims=True)
        off_hi = off.astype(BF16).astype(F32)
        tail = jnp.where(lane == 0, off_hi, jnp.where(lane == 1, off - off_hi, 0.0)).astype(BF16)
        t = dot(jnp.concatenate([a, tail], 1), ut_ref[...])
        ds = (e_ref[i].astype(F32) * t).astype(BF16)
        x = dot(ds, u2_ref[...])
        xs.append((x + pltpu.roll(x, vox, 1)) * (inv_ref[i] * factor))
    x = jnp.where(low_half((rows, pair), vox), xs[0], xs[1])
    hi, lo = split(x)
    r = dot(qt_ref[...], jnp.concatenate([hi, lo], 1))
    m_ref[:, here] = r[:vox, :pair] + r[vox:, :pair] + r[:vox, pair:]


def final_kernel(m_ref, n_ref, terms_ref, embed_t_ref, head_ref, qkv_ref, out_ref):
    vox = m_ref.shape[0]
    pair = 2 * vox
    embed_t = embed_t_ref[...].astype(F32)
    head = head_ref[...].astype(F32)
    left = low_half((vox, pair), vox)

    def row_form(m, e):
        return jnp.dot(m, jnp.concatenate(half_masks(e, vox), 0), precision=HIGH, preferred_element_type=F32)

    def col_form(m, e):
        both = dot_tn(m, e, HIGH)
        return jnp.where(left, both[:vox], both[vox:])

    def put(rows, t):
        return jnp.dot(rows, t, precision=HIGH, preferred_element_type=F32)

    for p in range(m_ref.shape[1] // pair):
        cols = slice(p * pair, (p + 1) * pair)
        m, n = m_ref[:, cols], n_ref[:, cols]
        qkv_ref[0, :, cols] = put(embed_t, row_form(m, terms_ref[1, :, cols]))
        qkv_ref[1, :, cols] = put(embed_t, col_form(m, terms_ref[0, :, cols]))
        qkv_ref[2, :, cols] = put(embed_t, col_form(n, terms_ref[3, :, cols]))
        out_ref[:, cols] = put(head, row_form(n, terms_ref[2, :, cols]))


def partner(shard, axis, apart):
    return lax.ppermute(shard, axis, [(i, i ^ 1 << apart) for i in range(lax.axis_size(axis))])


def sum_over(x, axis):
    for bit in range(lax.axis_size(axis).bit_length() - 1):
        x = x + partner(x, axis, bit)
    return x


def struct(shape, dtype):
    return jax.ShapeDtypeStruct(shape, dtype)


def whole(shape):
    return pl.BlockSpec(shape, lambda *_: (0,) * len(shape))


def per_device(volume, vox_mask, embed, w_qkv, w_out, w_head):
    rows, vox = volume.shape
    dim, width = w_qkv.shape[1:]
    heads = width // vox
    pair = 2 * vox
    steps = heads // 2
    head_dim = dim // HEADS
    factor = head_dim ** (-0.5)
    seq = lax.axis_size("seq")
    keys = (LEVELS + 1) * rows
    loss_weight = 256.0 / math.sqrt(rows * seq)

    kept = volume * (1 - vox_mask).astype(BF16)
    others = [partner(kept, "seq", bit) for bit in range(LEVELS)]

    b4, a2, ah, terms, own = pl.pallas_call(
        functools.partial(weights_kernel, factor * math.log2(math.e)),
        out_shape=(
            struct((4 * vox, 2 * width), BF16),
            struct((2 * vox, 2 * width), BF16),
            struct((2 * vox, width), BF16),
            struct((4, vox, width), F32),
            struct((2 * vox, vox), BF16),
        ),
        name="weights",
        compiler_params=pltpu.CompilerParams(vmem_limit_bytes=24 << 20),
    )(embed, w_qkv, w_out, w_head)

    e, c, inv, part, u2, qt = pl.pallas_call(
        forward_kernel,
        grid=(steps,),
        in_specs=[whole((rows, vox))] * 3
        + [whole((vox, dim)), whole((4 * vox, 2 * width)), whole((2 * vox, width))],
        out_specs=(
            pl.BlockSpec((2, rows, keys), lambda i: (i, 0, 0)),
            whole((rows, width)),
            pl.BlockSpec((2, rows, pair), lambda i: (i, 0, 0)),
            whole((rows, vox)),
            whole((keys, pair)),
            whole((pair, rows)),
        ),
        out_shape=(
            struct((heads, rows, keys), BF16),
            struct((rows, width), F32),
            struct((heads, rows, pair), F32),
            struct((rows, vox), F32),
            struct((keys, pair), BF16),
            struct((pair, rows), BF16),
        ),
        scratch_shapes=[
            pltpu.VMEM((pair, keys), BF16),
            pltpu.VMEM((keys, 2 * pair), BF16),
            pltpu.VMEM((rows, 2 * width), BF16),
        ],
        name="forward",
        compiler_params=pltpu.CompilerParams(vmem_limit_bytes=40 << 20),
    )(kept, *others, embed, b4, ah)

    other = partner(part, "head", 0)

    m, n = pl.pallas_call(
        functools.partial(backward_kernel, loss_weight, factor),
        grid=(steps,),
        in_specs=[whole((rows, vox))] * 5
        + [
            whole((pair, vox)),
            whole((pair, 2 * width)),
            whole((rows, width)),
            pl.BlockSpec((2, rows, pair), lambda i: (i, 0, 0)),
            pl.BlockSpec((2, rows, keys), lambda i: (i, 0, 0)),
            whole((keys, pair)),
            whole((pair, rows)),
        ],
        out_specs=(whole((vox, width)), whole((vox, width))),
        out_shape=(struct((vox, width), F32), struct((vox, width), F32)),
        scratch_shapes=[pltpu.VMEM((2 * pair, keys), BF16), pltpu.VMEM((rows, 2 * width), BF16)],
        name="backward",
        compiler_params=pltpu.CompilerParams(vmem_limit_bytes=40 << 20),
    )(part, other, volume, vox_mask, kept, own, a2, c, inv, e, u2, qt)

    n = sum_over(n, "seq")
    m = sum_over(m, "seq")

    piece = dim // seq
    start = lax.axis_index("seq") * piece
    embed_t = lax.dynamic_slice_in_dim(embed, start, piece, 1).T
    head_rows = lax.dynamic_slice_in_dim(w_head, start, piece, 0)
    return pl.pallas_call(
        final_kernel,
        out_shape=(struct((3, piece, width), F32), struct((piece, width), F32)),
        name="final",
    )(m, n, terms, embed_t, head_rows)


def solution(mesh):
    return jax.shard_map(
        per_device,
        mesh=mesh,
        in_specs=(P("seq", None), P("seq", None), P(), P(None, None, "head"), P(None, "head"), P()),
        out_specs=(P(None, "seq", "head"), P("seq", "head")),
        check_vma=False,
    )
```

time: 398 us -> 84.1 us (0.21)
  waiting for transfers between devices: 183 us -> 21.5 us
  matrix products: 132 us -> 0 us
  Pallas kernels: 0 us -> 35.3 us
  other arithmetic: 27 us -> 1.52 us
  local copies, waits for them, and re-layouts: 34.2 us -> 9.31 us
  between operations: 14.3 us -> 0.75 us
  starting transfers between devices: 4.87 us -> 15.5 us
    dot_general x65 -> x0, matrix products: 132 us -> none  [the longest x16 27.6 us: softmax_rows(): jnp.einsum('qd,kd->qk', query_head, key_head, preferred_element_type=jnp....]
    reduce_scatter x1 -> x0, waiting for transfers between devices: 104 us -> none  [per_device(): lax.psum_scatter(jnp.stack([query_term, key_term, value_term, out_term],...]
    psum x1 -> x0, waiting for transfers between devices: 41.5 us -> none  [per_device(): lax.psum(partial_out.astype(jnp.bfloat16), 'head').astype(jnp.float32)]
    pallas_call x0 -> x4, Pallas kernels: none -> 35.3 us  [the longest x1 15.6 us: per_device(): pl.pallas_call(forward_kernel, grid=(steps,), in_specs=[whole((rows, vox)...]
    reduce_sum x26 -> x0, other arithmetic: 18 us -> none  [the longest x16 9.12 us: softmax_rows(): return raised / jnp.sum(raised, -1, keepdims=True)]
    ppermute x4 -> x11, waiting for transfers between devices: 38.3 us -> 21.5 us  [partner(): lax.ppermute(shard, axis, [(i, i ^ 1 << apart) for i in range(lax.axis_si...]
    ppermute x4 -> x11, starting transfers between devices: 4.61 us -> 15.5 us  [partner(): lax.ppermute(shard, axis, [(i, i ^ 1 << apart) for i in range(lax.axis_si...]
    concatenate x6 -> x0, local copies, waits for them, and re-layouts: 9.6 us -> none  [the longest x3 5.19 us: per_device(): jnp.concatenate([projected[2]] + [other[1] for other in remote], 0)]
  transfers between devices with their start and end apart: 6 -> 11, of which waited for: 4 -> 8; matrix products, arithmetic and copies ran while one was open for 3% -> 4% of each run, Pallas kernels for 0% -> 2%
where the time goes in v1:
time: 84.1 us; the launch traced here: 83.9 us
  Pallas kernels  35.3 us (42%)
  waiting for transfers between devices  21.5 us (26%)
  starting transfers between devices  15.5 us (18%)
  local copies, waits for them, and re-layouts  9.31 us (11%)
  other arithmetic  1.52 us (2%)
    ppermute x11, waiting for transfers between devices, partner(): lax.ppermute(shard, axis, [(i, i ^ 1 << apart) for i in range(lax.axis_si...  21.5 us
    pallas_call x1, Pallas kernels, per_device(): pl.pallas_call(forward_kernel, grid=(steps,), in_specs=[whole((rows, vox)...  15.6 us
    ppermute x11, starting transfers between devices, partner(): lax.ppermute(shard, axis, [(i, i ^ 1 << apart) for i in range(lax.axis_si...  15.5 us
    pallas_call x1, Pallas kernels, per_device(): pl.pallas_call(functools.partial(backward_kernel, loss_weight, factor), g...  11.6 us
    unnamed x14, local copies, waits for them, and re-layouts  8.63 us
    pallas_call x1, Pallas kernels, per_device(): pl.pallas_call(final_kernel, out_shape=(struct((3, piece, width), F32), s...  6.28 us
    pallas_call x1, Pallas kernels, per_device(): pl.pallas_call(functools.partial(weights_kernel, factor * math.log2(math....  1.78 us
  transfers between devices with their start and end apart: 11, of which 8 were waited for; matrix products, arithmetic and copies ran while one was open for 4% of the time, Pallas kernels for 2%

profile of v1, /device:TPU:0, one launch (start us, length us, event | category | flops | bytes accessed | tf_op | source)
XLA Modules:
  0.0 83.9 jit_solution(9482808118653105050)
XLA Ops:
  0.6 0.0 copy-start.3
  0.6 1.0 %copy.9.vol_ref = bf16[512,64]{1,0:T(8,128)(2,1)S(1)} copy(bf16[512,64]{0,1:T(8,128)(2,1)} %param.6) | data formatting | bytes 131072 | tf_op args[0]
  1.6 1.0 %copy.8.mask_ref = s32[512,64]{1,0:T(8,128)S(1)} copy(s32[512,64]{0,1:T(8,128)} %param.7) | data formatting | bytes 262144 | tf_op args[1]
  2.7 3.1 %collective-permute-start.1 = (bf16[512,64]{1,0:T(8,128)(2,1)S(1)}, bf16[512,64]{1,0:T(8,128)(2,1)S(1)}, u32[]{:S(2)}, u32[]{:S(2)}) collective-permute-start(bf16[512,64]{1,0:T(8,128)(2,1)S(1)} %fusion.kept_ref), channel_id=1, source_target_pairs={{0,4},{2,6},{4,0},{6,2},{8,12},{10,14},{12,8},{14,10},{16,20},{18,... | collective-permute-start | bytes 196616 | tf_op jit(solution)/shard_map/ppermute | solution.py:211
  5.8 0.0 collective-permute-start
  5.8 1.1 %copy.10.w_head_ref = bf16[1024,64]{1,0:T(8,128)(2,1)S(1)} copy(bf16[1024,64]{0,1:T(8,128)(2,1)} %param.11) | data formatting | bytes 262144 | tf_op args[5]
  6.9 0.0 copy-start
  6.9 1.9 %copy-done = bf16[3,1024,512]{2,1,0:T(8,128)(2,1)S(1)} copy-done((bf16[3,1024,512]{2,1,0:T(8,128)(2,1)S(1)}, bf16[3,1024,512]{2,1,0:T(8,128)(2,1)}, u32[]{:S(2)}) %copy-start) | copy-done | bytes 3145752
  8.8 0.0 copy-start.1
  8.8 1.2 %copy-done.1 = bf16[1024,512]{1,0:T(8,128)(2,1)S(1)} copy-done((bf16[1024,512]{1,0:T(8,128)(2,1)S(1)}, bf16[1024,512]{1,0:T(8,128)(2,1)}, u32[]{:S(2)}) %copy-start.1) | copy-done | bytes 1048600
  10.0 0.0 copy-start.2
  10.0 0.9 %copy-done.2 = bf16[64,1024]{1,0:T(8,128)(2,1)S(1)} copy-done((bf16[64,1024]{1,0:T(8,128)(2,1)S(1)}, bf16[64,1024]{1,0:T(8,128)(2,1)}, u32[]{:S(2)}) %copy-start.2) | copy-done | bytes 131096
  10.9 1.8 %weights.1 = (bf16[256,1024]{1,0:T(8,128)(2,1)S(1)}, bf16[128,1024]{1,0:T(8,128)(2,1)S(1)}, bf16[128,512]{1,0:T(8,128)(2,1)S(1)}, f32[4,64,512]{2,1,0:T(8,128)S(1)}, bf16[128,64]{1,0:T(8,128)(2,1)S(1)}) custom-call(bf16[64,1024]{1,0:T(8,128)(2,1)S(1)} %copy-done.2, bf16[3,1024,512]{2,1,0:T(8,128)(2,1)S(1)} %copy-done, bf16[1024,512]{1,0:T(8,128)(2,1)S(1)} %copy-done.1, ...), custom_call_target="tpu_custom_call" | custom-call | tf_op jit(solution)/shard_map/weights/pallas_call | solution.py:243
  12.7 0.0 copy-start.4
  12.7 0.8 copy-done.4
  13.5 0.0 collective-permute-done.1.k2_ref
  13.5 0.0 collective-permute-done.k1_ref
  13.5 0.0 copy-done.3
  13.5 15.6 %forward.1 = (bf16[8,512,1536]{2,1,0:T(8,128)(2,1)}, f32[512,512]{1,0:T(8,128)S(1)}, f32[8,512,128]{2,1,0:T(8,128)S(1)}, f32[512,64]{1,0:T(8,128)S(1)}, bf16[153...) custom-call(bf16[512,64]{1,0:T(8,128)(2,1)S(1)} %fusion.kept_ref, bf16[512,64]{1,0:T(8,128)(2,1)S(1)} %collective-permute-done.k1_ref, ...), custom_call_target="tpu_custom_call" | custom-call | tf_op jit(solution)/shard_map/forward/pallas_call | solution.py:256
  29.1 1.5 %collective-permute-start.2 = (f32[512,64]{1,0:T(8,128)S(1)}, f32[512,64]{1,0:T(8,128)S(1)}, u32[]{:S(2)}, u32[]{:S(2)}) collective-permute-start(f32[512,64]{1,0:T(8,128)S(1)} %get-tuple-element.17.part_ref), channel_id=1, source_target_pairs={{0,1},{1,0},{2,3},{3,2},{4,5},{5,4},{6,7},{7,6},{8,9},{9,8},{10,11... | collective-permute-start | bytes 393224 | tf_op jit(solution)/shard_map/ppermute | solution.py:211
  30.6 7.2 %collective-permute-done.2.other_ref = f32[512,64]{1,0:T(8,128)S(1)} collective-permute-done((f32[512,64]{1,0:T(8,128)S(1)}, f32[512,64]{1,0:T(8,128)S(1)}, u32[]{:S(2)}, u32[]{:S(2)}) %collective-permute-start.2) | collective-permute-done | bytes 131104 | tf_op jit(solution)/shard_map/ppermute | solution.py:211
  37.8 11.6 %backward.1 = (f32[64,512]{1,0:T(8,128)S(1)}, f32[64,512]{1,0:T(8,128)S(1)}) custom-call(f32[512,64]{1,0:T(8,128)S(1)} %get-tuple-element.17.part_ref, f32[512,64]{1,0:T(8,128)S(1)} %collective-permute-done.2.other_ref, bf16[512,64]{1,0:T(8,128)(2,1)S(1)} %copy.9.vol_ref, s32[512,64]{1,0:T(8,128)S(1)} %copy.8.mask_ref, bf16[512,64]{1,0:T(8,128)(2,1)S(1)} %fusion.kept_ref, ...), custom_call_target="tpu_custom_call" | custom-call | tf_op jit(solution)/shard_map/backward/pallas_call | solution.py:288
  49.5 0.1 collective-permute-start.3
  49.5 0.5 collective-permute-start.7
  50.0 0.8 collective-permute-done.3
  50.9 0.3 collective-permute-start.4
  51.2 0.0 collective-permute-done.7
  51.3 1.8 %collective-permute-start.8 = (f32[64,512]{1,0:T(8,128)S(1)}, f32[64,512]{1,0:T(8,128)S(1)}, u32[]{:S(2)}, u32[]{:S(2)}) collective-permute-start(f32[64,512]{1,0:T(8,128)S(1)} %add.32), channel_id=1, source_target_pairs={{0,4},{2,6},{4,0},{6,2},{8,12},{10,14},{12,8},{14,10},{16,20},{18,... | collective-permute-start | bytes 393224 | tf_op jit(solution)/shard_map/ppermute | solution.py:211
  53.1 4.2 %collective-permute-done.4 = f32[64,512]{1,0:T(8,128)S(1)} collective-permute-done((f32[64,512]{1,0:T(8,128)S(1)}, f32[64,512]{1,0:T(8,128)S(1)}, u32[]{:S(2)}, u32[]{:S(2)}) %collective-permute-start.4) | collective-permute-done | bytes 131104 | tf_op jit(solution)/shard_map/ppermute | solution.py:211
  57.4 1.6 %collective-permute-start.5 = (f32[64,512]{1,0:T(8,128)S(1)}, f32[64,512]{1,0:T(8,128)S(1)}, u32[]{:S(2)}, u32[]{:S(2)}) collective-permute-start(f32[64,512]{1,0:T(8,128)S(1)} %add.29), channel_id=1, source_target_pairs={{0,8},{2,10},{4,12},{6,14},{8,0},{10,2},{12,4},{14,6},{16,24},{18,... | collective-permute-start | bytes 393224 | tf_op jit(solution)/shard_map/ppermute | solution.py:211
  59.0 0.3 collective-permute-done.8
  59.4 1.6 %collective-permute-start.9 = (f32[64,512]{1,0:T(8,128)S(1)}, f32[64,512]{1,0:T(8,128)S(1)}, u32[]{:S(2)}, u32[]{:S(2)}) collective-permute-start(f32[64,512]{1,0:T(8,128)S(1)} %add.33), channel_id=1, source_target_pairs={{0,8},{2,10},{4,12},{6,14},{8,0},{10,2},{12,4},{14,6},{16,24},{18,... | collective-permute-start | bytes 393224 | tf_op jit(solution)/shard_map/ppermute | solution.py:211
  61.0 2.5 %collective-permute-done.5 = f32[64,512]{1,0:T(8,128)S(1)} collective-permute-done((f32[64,512]{1,0:T(8,128)S(1)}, f32[64,512]{1,0:T(8,128)S(1)}, u32[]{:S(2)}, u32[]{:S(2)}) %collective-permute-start.5) | collective-permute-done | bytes 131104 | tf_op jit(solution)/shard_map/ppermute | solution.py:211
  63.5 2.6 %collective-permute-start.6 = (f32[64,512]{1,0:T(8,128)S(1)}, f32[64,512]{1,0:T(8,128)S(1)}, u32[]{:S(2)}, u32[]{:S(2)}) collective-permute-start(f32[64,512]{1,0:T(8,128)S(1)} %add.30), channel_id=1, source_target_pairs={{0,16},{2,18},{4,20},{6,22},{8,24},{10,26},{12,28},{14,30},{16,0},... | collective-permute-start | bytes 393224 | tf_op jit(solution)/shard_map/ppermute | solution.py:211
  66.2 0.5 collective-permute-done.9
  66.6 2.3 %collective-permute-start.10 = (f32[64,512]{1,0:T(8,128)S(1)}, f32[64,512]{1,0:T(8,128)S(1)}, u32[]{:S(2)}, u32[]{:S(2)}) collective-permute-start(f32[64,512]{1,0:T(8,128)S(1)} %add.34), channel_id=1, source_target_pairs={{0,16},{2,18},{4,20},{6,22},{8,24},{10,26},{12,28},{14,30},{16,0},... | collective-permute-start | bytes 393224 | tf_op jit(solution)/shard_map/ppermute | solution.py:211
  69.0 0.1 constant_dynamic-slice_fusion.1
  69.0 0.7 copy.15
  69.7 0.6 constant_dynamic-slice_fusion.head_ref
  70.3 4.4 %collective-permute-done.6 = f32[64,512]{1,0:T(8,128)S(1)} collective-permute-done((f32[64,512]{1,0:T(8,128)S(1)}, f32[64,512]{1,0:T(8,128)S(1)}, u32[]{:S(2)}, u32[]{:S(2)}) %collective-permute-start.6) | collective-permute-done | bytes 131104 | tf_op jit(solution)/shard_map/ppermute | solution.py:211
  74.8 0.7 add.31.m_ref
  75.5 1.4 %collective-permute-done.10 = f32[64,512]{1,0:T(8,128)S(1)} collective-permute-done((f32[64,512]{1,0:T(8,128)S(1)}, f32[64,512]{1,0:T(8,128)S(1)}, u32[]{:S(2)}, u32[]{:S(2)}) %collective-permute-start.10) | collective-permute-done | bytes 131104 | tf_op jit(solution)/shard_map/ppermute | solution.py:211
  76.9 0.7 add.35.n_ref
  77.6 6.3 %final.1 = (f32[3,64,512]{2,1,0:T(8,128)}, f32[64,512]{1,0:T(8,128)}) custom-call(f32[64,512]{1,0:T(8,128)} %add.31.m_ref, f32[64,512]{1,0:T(8,128)} %add.35.n_ref, f32[4,64,512]{2,1,0:T(8,128)} %copy-done.4, bf16[64,64]{1,0:T(8,128)(2,1)} %bitcast.1, bf16[64,64]{1,0:T(8,128)(2,1)} %constant_dynamic-slice_fusion.head_ref), custom_call_target="tpu_custom_call" | custom-call | tf_op jit(solution)/shard_map/final/pallas_call | solution.py:315
  (7 shorter events, 0.2 us)
Async XLA Ops:
  0.6 12.9 %copy-start.3 = (bf16[64,1024]{1,0:T(8,128)(2,1)S(1)}, bf16[64,1024]{1,0:T(8,128)(2,1)}, u32[]{:S(2)}) copy-start(bf16[64,1024]{1,0:T(8,128)(2,1)} %embed_ref.3) | copy-start | bytes 393220
  2.7 10.8 %collective-permute-start.1 = (bf16[512,64]{1,0:T(8,128)(2,1)S(1)}, bf16[512,64]{1,0:T(8,128)(2,1)S(1)}, u32[]{:S(2)}, u32[]{:S(2)}) collective-permute-start(bf16[512,64]{1,0:T(8,128)(2,1)S(1)} %fusion.kept_ref), channel_id=1, source_target_pairs={{0,4},{2,6},{4,0},{6,2},{8,12},{10,14},{12,8},{14,10},{16,20},{18,... | collective-permute-start | bytes 196616 | tf_op jit(solution)/shard_map/ppermute | solution.py:211
  5.8 7.7 %collective-permute-start = (bf16[512,64]{1,0:T(8,128)(2,1)S(1)}, bf16[512,64]{1,0:T(8,128)(2,1)S(1)}, u32[]{:S(2)}, u32[]{:S(2)}) collective-permute-start(bf16[512,64]{1,0:T(8,128)(2,1)S(1)} %fusion.kept_ref), channel_id=1, source_target_pairs={{0,2},{2,0},{4,6},{6,4},{8,10},{10,8},{12,14},{14,12},{16,18},{18,... | collective-permute-start | bytes 196616 | tf_op jit(solution)/shard_map/ppermute | solution.py:211
  6.9 1.9 %copy-start = (bf16[3,1024,512]{2,1,0:T(8,128)(2,1)S(1)}, bf16[3,1024,512]{2,1,0:T(8,128)(2,1)}, u32[]{:S(2)}) copy-start(bf16[3,1024,512]{2,1,0:T(8,128)(2,1)} %w_qkv_ref.1) | copy-start | bytes 9437188
  8.8 1.2 %copy-start.1 = (bf16[1024,512]{1,0:T(8,128)(2,1)S(1)}, bf16[1024,512]{1,0:T(8,128)(2,1)}, u32[]{:S(2)}) copy-start(bf16[1024,512]{1,0:T(8,128)(2,1)} %w_out_ref.1) | copy-start | bytes 3145732
  10.0 0.9 %copy-start.2 = (bf16[64,1024]{1,0:T(8,128)(2,1)S(1)}, bf16[64,1024]{1,0:T(8,128)(2,1)}, u32[]{:S(2)}) copy-start(bf16[64,1024]{1,0:T(8,128)(2,1)} %embed_ref.3) | copy-start | bytes 393220
  12.7 0.8 copy-start.4
  29.1 8.7 %collective-permute-start.2 = (f32[512,64]{1,0:T(8,128)S(1)}, f32[512,64]{1,0:T(8,128)S(1)}, u32[]{:S(2)}, u32[]{:S(2)}) collective-permute-start(f32[512,64]{1,0:T(8,128)S(1)} %get-tuple-element.17.part_ref), channel_id=1, source_target_pairs={{0,1},{1,0},{2,3},{3,2},{4,5},{5,4},{6,7},{7,6},{8,9},{9,8},{10,11... | collective-permute-start | bytes 393224 | tf_op jit(solution)/shard_map/ppermute | solution.py:211
  49.5 1.4 %collective-permute-start.3 = (f32[64,512]{1,0:T(8,128)S(1)}, f32[64,512]{1,0:T(8,128)S(1)}, u32[]{:S(2)}, u32[]{:S(2)}) collective-permute-start(f32[64,512]{1,0:T(8,128)S(1)} %get-tuple-element.25), channel_id=1, source_target_pairs={{0,2},{2,0},{4,6},{6,4},{8,10},{10,8},{12,14},{14,12},{16,18},{18,... | collective-permute-start | bytes 393224 | tf_op jit(solution)/shard_map/ppermute | solution.py:211
  49.5 1.7 %collective-permute-start.7 = (f32[64,512]{1,0:T(8,128)S(1)}, f32[64,512]{1,0:T(8,128)S(1)}, u32[]{:S(2)}, u32[]{:S(2)}) collective-permute-start(f32[64,512]{1,0:T(8,128)S(1)} %get-tuple-element.26), channel_id=1, source_target_pairs={{0,2},{2,0},{4,6},{6,4},{8,10},{10,8},{12,14},{14,12},{16,18},{18,... | collective-permute-start | bytes 393224 | tf_op jit(solution)/shard_map/ppermute | solution.py:211
  50.9 6.4 %collective-permute-start.4 = (f32[64,512]{1,0:T(8,128)S(1)}, f32[64,512]{1,0:T(8,128)S(1)}, u32[]{:S(2)}, u32[]{:S(2)}) collective-permute-start(f32[64,512]{1,0:T(8,128)S(1)} %add.28), channel_id=1, source_target_pairs={{0,4},{2,6},{4,0},{6,2},{8,12},{10,14},{12,8},{14,10},{16,20},{18,... | collective-permute-start | bytes 393224 | tf_op jit(solution)/shard_map/ppermute | solution.py:211
  51.3 8.1 %collective-permute-start.8 = (f32[64,512]{1,0:T(8,128)S(1)}, f32[64,512]{1,0:T(8,128)S(1)}, u32[]{:S(2)}, u32[]{:S(2)}) collective-permute-start(f32[64,512]{1,0:T(8,128)S(1)} %add.32), channel_id=1, source_target_pairs={{0,4},{2,6},{4,0},{6,2},{8,12},{10,14},{12,8},{14,10},{16,20},{18,... | collective-permute-start | bytes 393224 | tf_op jit(solution)/shard_map/ppermute | solution.py:211
  57.4 6.1 %collective-permute-start.5 = (f32[64,512]{1,0:T(8,128)S(1)}, f32[64,512]{1,0:T(8,128)S(1)}, u32[]{:S(2)}, u32[]{:S(2)}) collective-permute-start(f32[64,512]{1,0:T(8,128)S(1)} %add.29), channel_id=1, source_target_pairs={{0,8},{2,10},{4,12},{6,14},{8,0},{10,2},{12,4},{14,6},{16,24},{18,... | collective-permute-start | bytes 393224 | tf_op jit(solution)/shard_map/ppermute | solution.py:211
  59.4 7.3 %collective-permute-start.9 = (f32[64,512]{1,0:T(8,128)S(1)}, f32[64,512]{1,0:T(8,128)S(1)}, u32[]{:S(2)}, u32[]{:S(2)}) collective-permute-start(f32[64,512]{1,0:T(8,128)S(1)} %add.33), channel_id=1, source_target_pairs={{0,8},{2,10},{4,12},{6,14},{8,0},{10,2},{12,4},{14,6},{16,24},{18,... | collective-permute-start | bytes 393224 | tf_op jit(solution)/shard_map/ppermute | solution.py:211
  63.5 11.3 %collective-permute-start.6 = (f32[64,512]{1,0:T(8,128)S(1)}, f32[64,512]{1,0:T(8,128)S(1)}, u32[]{:S(2)}, u32[]{:S(2)}) collective-permute-start(f32[64,512]{1,0:T(8,128)S(1)} %add.30), channel_id=1, source_target_pairs={{0,16},{2,18},{4,20},{6,22},{8,24},{10,26},{12,28},{14,30},{16,0},... | collective-permute-start | bytes 393224 | tf_op jit(solution)/shard_map/ppermute | solution.py:211
  66.6 10.3 %collective-permute-start.10 = (f32[64,512]{1,0:T(8,128)S(1)}, f32[64,512]{1,0:T(8,128)S(1)}, u32[]{:S(2)}, u32[]{:S(2)}) collective-permute-start(f32[64,512]{1,0:T(8,128)S(1)} %add.34), channel_id=1, source_target_pairs={{0,16},{2,18},{4,20},{6,22},{8,24},{10,26},{12,28},{14,30},{16,0},... | collective-permute-start | bytes 393224 | tf_op jit(solution)/shard_map/ppermute | solution.py:211
